TPU v7x, 128 devices: a whole 4x4x4 slice. The times are simulated.
128 devices in a mesh: section: 4 (over x), dp: 32 (over y, z, core).
Axes of the slice: x: 4, y: 4, z: 4, core: 2. Of those that a mesh axis runs over, the one named last changes fastest.
Arguments:
- tokens: bfloat16 [4096, 8192], P('dp'), may hold values from -6 to 6
- cotangent: bfloat16 [4096, 8192], P('dp'), may hold values from -6 to 6
- gains: float32 [4, 8192], P('section'), may hold values from 0.5 to 1.5
- value_projection_weight: bfloat16 [4, 8192, 1024], P('section', 'dp'), may hold values from -0.0625 to 0.0625
- output_projection_weight: bfloat16 [4, 8192, 1024], P('section', 'dp'), may hold values from -0.1875 to 0.1875
- block_adapter_ids: int32 [32], replicated, may hold values from 0 to 63
- job_adapter: int32 [32, 64], replicated, may hold values from -1 to 63, as said below
- job_slab: int32 [32, 64], replicated, may hold values from -1 to 15, as said below
- token_counts: int32 [64], replicated, may hold values from 128 to 1023
- slot_adapter_params: bfloat16 [4, 2048, 9216], P('section', 'dp'), may hold values from -0.29882812 to 0.29882812
- first_moment: float32 [4, 2048, 9216], P('section', 'dp'), may hold values from -6 to 6
- second_moment: float32 [4, 2048, 9216], P('section', 'dp'), may hold values from 0.1 to 10
Outputs:
- new_params: bfloat16 [4, 2048, 9216], P('section', 'dp')
- new_first: float32 [4, 2048, 9216], P('section', 'dp')
- new_second: float32 [4, 2048, 9216], P('section', 'dp')
- user_panels: bfloat16 [4, 32, 147456], P('section', 'dp')
Inputs may be any that keep to these rules, and one draw needn't show every extreme that they name: `job_adapter`: row o lists the adapters of which owner o holds a slab, each once, followed by -1; the 16 slabs of every adapter are held by 16 different owners, and every slab of every adapter is held exactly once. `job_slab`: the slab held in the same entry of job_adapter; -1 exactly where job_adapter is -1.
All inputs are finite; a program needn't handle non-finite values.
Results may differ from a plain program's by a relative error of at most 0.001.
Values may be sent and summed in bfloat16 or wider, within the bound.
No kernel may reach another device: no remote copies, remote signals or barrier semaphores. Data moves between devices by JAX's collectives and lax.ppermute only.
A program may use at most 128 MiB of HBM per device.

v0:
```python
import jax
import jax.numpy as jnp
from jax import lax
from jax.sharding import PartitionSpec as P

ADAPTER_RANK = 16
MROWS = 16
ADAPTER_SCALE = 2.0
LEARN_RATE = 0.001
BETA_FIRST = 0.9
BETA_SECOND = 0.999
ADAM_EPS = 1e-08
FIRST_FIX = 1.0 - 0.9**50 * 0.9**50
SECOND_FIX = 1.0 - 0.999**50 * 0.999**50
NORM_EPS = 1e-05


def from_behind(shard, axis, by):
    length = lax.axis_size(axis)
    pairs = [(i, i + by) for i in range(length) if 0 <= i + by < length]
    return lax.ppermute(shard, axis, pairs)


def contract_trailing(left, right):
    return lax.dot_general(
        left, right, (((1,), (1,)), ((), ())), preferred_element_type=jnp.float32
    )


def contract_leading(left, right):
    return lax.dot_general(
        left, right, (((0,), (0,)), ((), ())), preferred_element_type=jnp.float32
    )


def norm_rows(hidden_state, gain_vector_row):
    hidden_wide = hidden_state.astype(jnp.float32)
    mean_square = jnp.mean(hidden_wide * hidden_wide, axis=-1, keepdims=True)
    norm_gain_scale = lax.rsqrt(mean_square + NORM_EPS)
    normalized_rows = (hidden_wide * norm_gain_scale * gain_vector_row).astype(jnp.bfloat16)
    return (hidden_wide, norm_gain_scale, normalized_rows)


def layer_ahead_pass(
    hidden_state, gain_vector_row, value_complete, output_complete, adapter_down, adapter_up
):
    hidden_wide, norm_gain_scale, normalized_rows = norm_rows(hidden_state, gain_vector_row)
    rank_projected = jnp.dot(
        normalized_rows, adapter_down, preferred_element_type=jnp.float32
    ).astype(jnp.bfloat16)
    value_block_rows = (
        jnp.dot(normalized_rows, value_complete, preferred_element_type=jnp.float32)
        + ADAPTER_SCALE * jnp.dot(rank_projected, adapter_up, preferred_element_type=jnp.float32)
    ).astype(jnp.bfloat16)
    output_block_rows = (hidden_wide + contract_trailing(value_block_rows, output_complete)).astype(
        jnp.bfloat16
    )
    return (output_block_rows, norm_gain_scale, normalized_rows, rank_projected)


def layer_reverse_pass(
    output_gradient,
    hidden_state,
    norm_gain_scale,
    normalized_rows,
    rank_projected,
    gain_vector_row,
    value_complete,
    output_complete,
    adapter_down,
    adapter_up,
):
    value_gradient = jnp.dot(
        output_gradient, output_complete, preferred_element_type=jnp.float32
    ).astype(jnp.bfloat16)
    low_rank_gradient = (ADAPTER_SCALE * contract_trailing(value_gradient, adapter_up)).astype(
        jnp.bfloat16
    )
    down_gradient = contract_leading(normalized_rows, low_rank_gradient)
    up_gradient = ADAPTER_SCALE * contract_leading(rank_projected, value_gradient)
    normed_gradient = (
        contract_trailing(value_gradient, value_complete)
        + contract_trailing(low_rank_gradient, adapter_down)
    ) * gain_vector_row
    hidden_wide = hidden_state.astype(jnp.float32)
    centred = jnp.mean(hidden_wide * normed_gradient, axis=-1, keepdims=True)
    grad_in = (
        output_gradient.astype(jnp.float32)
        + norm_gain_scale * normed_gradient
        - hidden_wide * norm_gain_scale**3 * centred
    )
    return (grad_in.astype(jnp.bfloat16), down_gradient, up_gradient)


def adam_update(params_old, first_old, second_old, slot_grad, live):
    first_step = BETA_FIRST * first_old + (1.0 - BETA_FIRST) * slot_grad
    second_step = BETA_SECOND * second_old + (1.0 - BETA_SECOND) * slot_grad * slot_grad
    step_size = first_step / FIRST_FIX / (jnp.sqrt(second_step / SECOND_FIX) + ADAM_EPS)
    params_step = (params_old.astype(jnp.float32) - LEARN_RATE * step_size).astype(jnp.bfloat16)
    return (
        jnp.where(live, params_step, params_old),
        jnp.where(live, first_step, first_old),
        jnp.where(live, second_step, second_old),
    )


def put_slot(saved_array, new_value, slot_number, is_valid):
    current = lax.dynamic_index_in_dim(saved_array, slot_number, 0, keepdims=False)
    return lax.dynamic_update_index_in_dim(
        saved_array, jnp.where(is_valid, new_value, current), slot_number, 0
    )


def select_slot(saved_array, slot_number):
    return lax.dynamic_index_in_dim(saved_array, slot_number, 0, keepdims=False)


def on_device(
    tokens,
    cotangent,
    gains,
    value_projection_weight,
    output_projection_weight,
    block_adapter_ids,
    job_adapter,
    job_slab,
    token_counts,
    slot_adapter_params,
    first_moment,
    second_moment,
):
    section_index = lax.axis_index("section")
    owner_index = lax.axis_index("dp")
    section_total = lax.axis_size("section")
    owner_total = lax.axis_size("dp")
    tok_dev, hidden_width = tokens.shape
    value_feature_width = value_projection_weight.shape[2]
    panel_width = slot_adapter_params.shape[2]
    slab_count = owner_total // 2
    block_total = block_adapter_ids.shape[0]
    local_blocks = block_total // owner_total
    block_rows = tok_dev // local_blocks
    adapter_total = token_counts.shape[0]
    divide_position = hidden_width * ADAPTER_RANK
    value_complete, output_complete = (
        lax.all_gather(value_projection_weight, "dp", axis=1, tiled=True),
        lax.all_gather(output_projection_weight, "dp", axis=1, tiled=True),
    )
    value_complete = value_complete[0]
    output_complete = output_complete[0]
    gain_vector_row = gains[0]
    my_jobs = lax.dynamic_index_in_dim(job_adapter, owner_index, 0, keepdims=False)
    my_blocks = lax.dynamic_slice_in_dim(
        block_adapter_ids, owner_index * local_blocks, local_blocks
    )
    slab_ids = jnp.arange(slab_count, dtype=jnp.int32)
    matching = (job_adapter[None, None] == my_blocks[:, None, None, None]) & (
        job_slab[None, None] == slab_ids[None, :, None, None]
    )
    owner_ids = jnp.arange(owner_total, dtype=jnp.int32)
    source_owner = jnp.sum(jnp.where(matching, owner_ids[None, None, :, None], 0), axis=(2, 3))
    own_select = (block_adapter_ids[:, None] == my_jobs[None, :]) & (my_jobs[None, :] >= 0)
    slot_rows = jnp.arange(local_blocks, dtype=jnp.int32)[:, None]

    def hand_out(owned):
        picked = jnp.dot(own_select.astype(jnp.bfloat16), owned, preferred_element_type=jnp.float32)
        return picked.astype(jnp.bfloat16).reshape(owner_total, local_blocks, panel_width)

    def assemble(arrived):
        gathered_slabs = arrived[source_owner, slot_rows]
        return gathered_slabs.reshape(local_blocks, slab_count * panel_width)

    gathered_panels = assemble(
        lax.all_to_all(
            hand_out(slot_adapter_params[0]), "dp", split_axis=0, concat_axis=0, tiled=True
        )
    )
    adapter_down_every = gathered_panels[:, :divide_position].reshape(
        local_blocks, hidden_width, ADAPTER_RANK
    )
    adapter_up_every = gathered_panels[:, divide_position:].reshape(
        local_blocks, ADAPTER_RANK, value_feature_width
    )
    micro_rows = MROWS
    micro_count = tok_dev // micro_rows
    per_block = block_rows // micro_rows
    step_count = section_total + micro_count - 1
    token_micro = tokens.reshape(micro_count, micro_rows, hidden_width)
    cot_micro = cotangent.reshape(micro_count, micro_rows, hidden_width)

    def forward_step(state_tuple, step_number):
        incoming, saved_in, saved_scale, saved_normed, saved_low = state_tuple
        micro_index = step_number - section_index
        is_valid = (micro_index >= 0) & (micro_index < micro_count)
        micro_slot = jnp.clip(micro_index, 0, micro_count - 1)
        hidden_state = jnp.where(section_index == 0, select_slot(token_micro, micro_slot), incoming)
        block_slot_index = micro_slot // per_block

        def forward_run_layer(unused):
            return layer_ahead_pass(
                hidden_state,
                gain_vector_row,
                value_complete,
                output_complete,
                select_slot(adapter_down_every, block_slot_index),
                select_slot(adapter_up_every, block_slot_index),
            )

        def forward_skip_layer(unused):
            return (
                jnp.zeros((micro_rows, hidden_width), jnp.bfloat16),
                jnp.zeros((micro_rows, 1), jnp.float32),
                jnp.zeros((micro_rows, hidden_width), jnp.bfloat16),
                jnp.zeros((micro_rows, ADAPTER_RANK), jnp.bfloat16),
            )

        output_block_rows, norm_gain_scale, normalized_rows, rank_projected = lax.cond(
            is_valid, forward_run_layer, forward_skip_layer, None
        )
        saved_in = put_slot(saved_in, hidden_state, micro_slot, is_valid)
        saved_scale = put_slot(saved_scale, norm_gain_scale, micro_slot, is_valid)
        saved_normed = put_slot(saved_normed, normalized_rows, micro_slot, is_valid)
        saved_low = put_slot(saved_low, rank_projected, micro_slot, is_valid)
        passed = from_behind(output_block_rows, "section", 1)
        return ((passed, saved_in, saved_scale, saved_normed, saved_low), None)

    forward_init = (
        jnp.zeros((micro_rows, hidden_width), jnp.bfloat16),
        jnp.zeros((micro_count, micro_rows, hidden_width), jnp.bfloat16),
        jnp.zeros((micro_count, micro_rows, 1), jnp.float32),
        jnp.zeros((micro_count, micro_rows, hidden_width), jnp.bfloat16),
        jnp.zeros((micro_count, micro_rows, ADAPTER_RANK), jnp.bfloat16),
    )
    forward_done, _ = lax.scan(forward_step, forward_init, jnp.arange(step_count, dtype=jnp.int32))
    _, saved_in, saved_scale, saved_normed, saved_low = forward_done

    def backward_step(state_tuple, step_number):
        incoming, block_grads = state_tuple
        micro_index = step_number - (section_total - 1 - section_index)
        is_valid = (micro_index >= 0) & (micro_index < micro_count)
        micro_slot = jnp.clip(micro_index, 0, micro_count - 1)
        output_gradient = jnp.where(
            section_index == section_total - 1, select_slot(cot_micro, micro_slot), incoming
        )
        block_slot_index = micro_slot // per_block

        def backward_run_layer(unused):
            return layer_reverse_pass(
                output_gradient,
                select_slot(saved_in, micro_slot),
                select_slot(saved_scale, micro_slot),
                select_slot(saved_normed, micro_slot),
                select_slot(saved_low, micro_slot),
                gain_vector_row,
                value_complete,
                output_complete,
                select_slot(adapter_down_every, block_slot_index),
                select_slot(adapter_up_every, block_slot_index),
            )

        def backward_skip_layer(unused):
            return (
                jnp.zeros((micro_rows, hidden_width), jnp.bfloat16),
                jnp.zeros((hidden_width, ADAPTER_RANK), jnp.float32),
                jnp.zeros((ADAPTER_RANK, value_feature_width), jnp.float32),
            )

        grad_in, down_gradient, up_gradient = lax.cond(
            is_valid, backward_run_layer, backward_skip_layer, None
        )
        grad_term = jnp.concatenate([down_gradient.reshape(-1), up_gradient.reshape(-1)])
        block_grads = block_grads.at[block_slot_index].add(jnp.where(is_valid, grad_term, 0.0))
        passed = from_behind(grad_in, "section", -1)
        return ((passed, block_grads), None)

    backward_init = (
        jnp.zeros((micro_rows, hidden_width), jnp.bfloat16),
        jnp.zeros((local_blocks, slab_count * panel_width), jnp.float32),
    )
    backward_done, _ = lax.scan(
        backward_step, backward_init, jnp.arange(step_count, dtype=jnp.int32)
    )
    block_grads = backward_done[1]
    outgoing = (
        jnp.zeros((owner_total, local_blocks, panel_width), jnp.float32)
        .at[source_owner, slot_rows]
        .set(block_grads.reshape(local_blocks, slab_count, panel_width))
    )
    arrived = lax.all_to_all(
        outgoing.astype(jnp.bfloat16), "dp", split_axis=0, concat_axis=0, tiled=True
    ).astype(outgoing.dtype)
    summed = jnp.dot(
        own_select.astype(jnp.float32).T,
        arrived.reshape(block_total, panel_width),
        precision=lax.Precision.HIGHEST,
        preferred_element_type=jnp.float32,
    )
    live = my_jobs >= 0
    adapter_ids = jnp.arange(adapter_total, dtype=jnp.int32)
    slot_counts = jnp.sum(
        jnp.where(adapter_ids[None, :] == my_jobs[:, None], token_counts[None, :], 0), axis=1
    )
    slot_counts = jnp.where(live, slot_counts, 1)
    slot_grad = summed / slot_counts.astype(jnp.float32)[:, None]
    params_new, first_new, second_new = adam_update(
        slot_adapter_params[0], first_moment[0], second_moment[0], slot_grad, live[:, None]
    )
    returned = assemble(
        lax.all_to_all(hand_out(params_new), "dp", split_axis=0, concat_axis=0, tiled=True)
    )
    return (params_new[None], first_new[None], second_new[None], returned[None])


def solution(mesh):
    return jax.shard_map(
        on_device,
        mesh=mesh,
        in_specs=(
            P("dp", None),
            P("dp", None),
            P("section", None),
            P("section", "dp", None),
            P("section", "dp", None),
            P(),
            P(),
            P(),
            P(),
            P("section", "dp", None),
            P("section", "dp", None),
            P("section", "dp", None),
        ),
        out_specs=(
            P("section", "dp", None),
            P("section", "dp", None),
            P("section", "dp", None),
            P("section", "dp", None),
        ),
        check_vma=False,
    )
```

profile of v0, /device:TPU:1, one launch (start us, length us, event | category | flops | bytes accessed | tf_op | source)
XLA Modules:
  0.0 1005.0 jit_solution(1554221455761827771)
XLA Ops:
  27.1 15.2 %all-to-all-done = bf16[32,2,4608]{2,1,0:T(2,128)(2,1)S(1)} async-done(((bf16[32,2,4608]{2,1,0:T(2,128)(2,1)}), bf16[32,2,4608]{2,1,0:T(2,128)(2,1)S(1)}, u32[]{:S(2)}, u32[]{:S(2)}) %all-to-all-start) | async-done | bytes 589856 | tf_op jit(solution)/shard_map/all_to_all | solution.py:174
  48.8 42.8 %all-gather.3.cloned.1.call-done = bf16[1,8192,1024]{2,1,0:T(8,128)(2,1)} async-done(((bf16[1,256,1024]{2,1,0:T(8,128)(2,1)}), bf16[1,8192,1024]{2,1,0:T(8,128)(2,1)}) %all-gather.3.cloned.1.call-update) | async-done | bytes 16777232 | tf_op jit(solution)/shard_map/all_gather | solution.py:146
  91.6 74.4 %all-gather.5.cloned.1.call-done = bf16[1,8192,1024]{2,1,0:T(8,128)(2,1)} async-done(((bf16[1,256,1024]{2,1,0:T(8,128)(2,1)}), bf16[1,8192,1024]{2,1,0:T(8,128)(2,1)}) %all-gather.5.cloned.1.call-update) | async-done | bytes 16777232 | tf_op jit(solution)/shard_map/all_gather | solution.py:147
  169.0 320.4 %while.36 = (s32[]{:T(128)}, bf16[16,8192]{1,0:T(8,128)(2,1)S(1)}, bf16[8,16,8192]{2,1,0:T(8,128)(2,1)}, f32[8,16,1]{1,2,0:T(1,128)S(1)}, bf16[8,16,8192]{2,1,0:...) while((s32[]{:T(128)}, bf16[16,8192]{1,0:T(8,128)(2,1)S(1)}, ...), condition=%wide.region_5.6_spmd, body=%wide.region_1.5_spmd.sunk | while | flops 543343104 | bytes 42153352 | solution.py:234
  173.0 19.6 %conditional.5 = (bf16[16,8192]{1,0:T(8,128)(2,1)S(1)}, f32[16,1]{0,1:T(1,128)S(1)}, bf16[16,8192]{1,0:T(8,128)(2,1)S(1)}, bf16[16,16]{1,0:T(8,128)(2,1)}) conditional(s32[]{:T(128)} %convert_element_type.134, () %tuple.117, (bf16[16,8192]{1,0:T(8,128)(2,1)S(1)}, f32[1,8192]{1,0:T(1,128)S(1)}, bf16[8192,1024]{1,0:T(8,128)(2,1)}, ...), branch_computations={%region_2.2_spmd, %region_3.4_spmd} | conditional | flops 542949632 | bytes 37946776 | solution.py:217
  182.3 10.3 %fusion = bf16[16,8192]{1,0:T(8,128)(2,1)S(1)} fusion(bf16[8192,1024]{1,0:T(8,128)(2,1)} %get-tuple-element.485, f32[16,1024]{1,0:T(8,128)S(1)} %fusion.58, bf16[16,16]{1,0:T(8,128)(2,1)} %convolution_convert_fusion, bf16[16,8192]{1,0:T(8,128)(2,1)S(1)} %get-tuple-element.480, bf16[1,16,1024]{2,1,0:T(8,128)(2,1)S(1)} %get-tuple-element.484), kind=kOutput, calls=%fused_computation.4 | convolution fusion | flops 269402112 | bytes 17400320 | tf_op jit(solution)/shard_map/while/body/eval_jaxpr/cond/branch_1_fun/dot_general | solution.py:25
  203.6 19.6 %conditional.5 = (bf16[16,8192]{1,0:T(8,128)(2,1)S(1)}, f32[16,1]{0,1:T(1,128)S(1)}, bf16[16,8192]{1,0:T(8,128)(2,1)S(1)}, bf16[16,16]{1,0:T(8,128)(2,1)}) conditional(s32[]{:T(128)} %convert_element_type.134, () %tuple.117, (bf16[16,8192]{1,0:T(8,128)(2,1)S(1)}, f32[1,8192]{1,0:T(1,128)S(1)}, bf16[8192,1024]{1,0:T(8,128)(2,1)}, ...), branch_computations={%region_2.2_spmd, %region_3.4_spmd} | conditional | flops 542949632 | bytes 37946776 | solution.py:217
  212.8 10.3 %fusion = bf16[16,8192]{1,0:T(8,128)(2,1)S(1)} fusion(bf16[8192,1024]{1,0:T(8,128)(2,1)} %get-tuple-element.485, f32[16,1024]{1,0:T(8,128)S(1)} %fusion.58, bf16[16,16]{1,0:T(8,128)(2,1)} %convolution_convert_fusion, bf16[16,8192]{1,0:T(8,128)(2,1)S(1)} %get-tuple-element.480, bf16[1,16,1024]{2,1,0:T(8,128)(2,1)S(1)} %get-tuple-element.484), kind=kOutput, calls=%fused_computation.4 | convolution fusion | flops 269402112 | bytes 17400320 | tf_op jit(solution)/shard_map/while/body/eval_jaxpr/cond/branch_1_fun/dot_general | solution.py:25
  236.0 19.6 %conditional.5 = (bf16[16,8192]{1,0:T(8,128)(2,1)S(1)}, f32[16,1]{0,1:T(1,128)S(1)}, bf16[16,8192]{1,0:T(8,128)(2,1)S(1)}, bf16[16,16]{1,0:T(8,128)(2,1)}) conditional(s32[]{:T(128)} %convert_element_type.134, () %tuple.117, (bf16[16,8192]{1,0:T(8,128)(2,1)S(1)}, f32[1,8192]{1,0:T(1,128)S(1)}, bf16[8192,1024]{1,0:T(8,128)(2,1)}, ...), branch_computations={%region_2.2_spmd, %region_3.4_spmd} | conditional | flops 542949632 | bytes 37946776 | solution.py:217
  245.3 10.3 %fusion = bf16[16,8192]{1,0:T(8,128)(2,1)S(1)} fusion(bf16[8192,1024]{1,0:T(8,128)(2,1)} %get-tuple-element.485, f32[16,1024]{1,0:T(8,128)S(1)} %fusion.58, bf16[16,16]{1,0:T(8,128)(2,1)} %convolution_convert_fusion, bf16[16,8192]{1,0:T(8,128)(2,1)S(1)} %get-tuple-element.480, bf16[1,16,1024]{2,1,0:T(8,128)(2,1)S(1)} %get-tuple-element.484), kind=kOutput, calls=%fused_computation.4 | convolution fusion | flops 269402112 | bytes 17400320 | tf_op jit(solution)/shard_map/while/body/eval_jaxpr/cond/branch_1_fun/dot_general | solution.py:25
  267.7 19.6 %conditional.5 = (bf16[16,8192]{1,0:T(8,128)(2,1)S(1)}, f32[16,1]{0,1:T(1,128)S(1)}, bf16[16,8192]{1,0:T(8,128)(2,1)S(1)}, bf16[16,16]{1,0:T(8,128)(2,1)}) conditional(s32[]{:T(128)} %convert_element_type.134, () %tuple.117, (bf16[16,8192]{1,0:T(8,128)(2,1)S(1)}, f32[1,8192]{1,0:T(1,128)S(1)}, bf16[8192,1024]{1,0:T(8,128)(2,1)}, ...), branch_computations={%region_2.2_spmd, %region_3.4_spmd} | conditional | flops 542949632 | bytes 37946776 | solution.py:217
  276.9 10.3 %fusion = bf16[16,8192]{1,0:T(8,128)(2,1)S(1)} fusion(bf16[8192,1024]{1,0:T(8,128)(2,1)} %get-tuple-element.485, f32[16,1024]{1,0:T(8,128)S(1)} %fusion.58, bf16[16,16]{1,0:T(8,128)(2,1)} %convolution_convert_fusion, bf16[16,8192]{1,0:T(8,128)(2,1)S(1)} %get-tuple-element.480, bf16[1,16,1024]{2,1,0:T(8,128)(2,1)S(1)} %get-tuple-element.484), kind=kOutput, calls=%fused_computation.4 | convolution fusion | flops 269402112 | bytes 17400320 | tf_op jit(solution)/shard_map/while/body/eval_jaxpr/cond/branch_1_fun/dot_general | solution.py:25
  298.6 19.6 %conditional.5 = (bf16[16,8192]{1,0:T(8,128)(2,1)S(1)}, f32[16,1]{0,1:T(1,128)S(1)}, bf16[16,8192]{1,0:T(8,128)(2,1)S(1)}, bf16[16,16]{1,0:T(8,128)(2,1)}) conditional(s32[]{:T(128)} %convert_element_type.134, () %tuple.117, (bf16[16,8192]{1,0:T(8,128)(2,1)S(1)}, f32[1,8192]{1,0:T(1,128)S(1)}, bf16[8192,1024]{1,0:T(8,128)(2,1)}, ...), branch_computations={%region_2.2_spmd, %region_3.4_spmd} | conditional | flops 542949632 | bytes 37946776 | solution.py:217
  307.9 10.3 %fusion = bf16[16,8192]{1,0:T(8,128)(2,1)S(1)} fusion(bf16[8192,1024]{1,0:T(8,128)(2,1)} %get-tuple-element.485, f32[16,1024]{1,0:T(8,128)S(1)} %fusion.58, bf16[16,16]{1,0:T(8,128)(2,1)} %convolution_convert_fusion, bf16[16,8192]{1,0:T(8,128)(2,1)S(1)} %get-tuple-element.480, bf16[1,16,1024]{2,1,0:T(8,128)(2,1)S(1)} %get-tuple-element.484), kind=kOutput, calls=%fused_computation.4 | convolution fusion | flops 269402112 | bytes 17400320 | tf_op jit(solution)/shard_map/while/body/eval_jaxpr/cond/branch_1_fun/dot_general | solution.py:25
  329.3 19.6 %conditional.5 = (bf16[16,8192]{1,0:T(8,128)(2,1)S(1)}, f32[16,1]{0,1:T(1,128)S(1)}, bf16[16,8192]{1,0:T(8,128)(2,1)S(1)}, bf16[16,16]{1,0:T(8,128)(2,1)}) conditional(s32[]{:T(128)} %convert_element_type.134, () %tuple.117, (bf16[16,8192]{1,0:T(8,128)(2,1)S(1)}, f32[1,8192]{1,0:T(1,128)S(1)}, bf16[8192,1024]{1,0:T(8,128)(2,1)}, ...), branch_computations={%region_2.2_spmd, %region_3.4_spmd} | conditional | flops 542949632 | bytes 37946776 | solution.py:217
  360.0 19.6 %conditional.5 = (bf16[16,8192]{1,0:T(8,128)(2,1)S(1)}, f32[16,1]{0,1:T(1,128)S(1)}, bf16[16,8192]{1,0:T(8,128)(2,1)S(1)}, bf16[16,16]{1,0:T(8,128)(2,1)}) conditional(s32[]{:T(128)} %convert_element_type.134, () %tuple.117, (bf16[16,8192]{1,0:T(8,128)(2,1)S(1)}, f32[1,8192]{1,0:T(1,128)S(1)}, bf16[8192,1024]{1,0:T(8,128)(2,1)}, ...), branch_computations={%region_2.2_spmd, %region_3.4_spmd} | conditional | flops 542949632 | bytes 37946776 | solution.py:217
  390.7 19.6 %conditional.5 = (bf16[16,8192]{1,0:T(8,128)(2,1)S(1)}, f32[16,1]{0,1:T(1,128)S(1)}, bf16[16,8192]{1,0:T(8,128)(2,1)S(1)}, bf16[16,16]{1,0:T(8,128)(2,1)}) conditional(s32[]{:T(128)} %convert_element_type.134, () %tuple.117, (bf16[16,8192]{1,0:T(8,128)(2,1)S(1)}, f32[1,8192]{1,0:T(1,128)S(1)}, bf16[8192,1024]{1,0:T(8,128)(2,1)}, ...), branch_computations={%region_2.2_spmd, %region_3.4_spmd} | conditional | flops 542949632 | bytes 37946776 | solution.py:217
  422.0 22.7 %collective-permute-start = (bf16[16,8192]{1,0:T(8,128)(2,1)S(1)}, bf16[16,8192]{1,0:T(8,128)(2,1)S(1)}, u32[]{:S(2)}, u32[]{:S(2)}) collective-permute-start(bf16[16,8192]{1,0:T(8,128)(2,1)S(1)} %get-tuple-element.992), channel_id=1, source_target_pairs={{0,32},{32,64},{64,96},{1,33},{33,65},{65,97},{2,34},{34,66},{66,9... | collective-permute-start | bytes 786440 | tf_op jit(solution)/shard_map/while/body/eval_jaxpr/ppermute | solution.py:21
  464.4 21.8 %collective-permute-start = (bf16[16,8192]{1,0:T(8,128)(2,1)S(1)}, bf16[16,8192]{1,0:T(8,128)(2,1)S(1)}, u32[]{:S(2)}, u32[]{:S(2)}) collective-permute-start(bf16[16,8192]{1,0:T(8,128)(2,1)S(1)} %get-tuple-element.992), channel_id=1, source_target_pairs={{0,32},{32,64},{64,96},{1,33},{33,65},{65,97},{2,34},{34,66},{66,9... | collective-permute-start | bytes 786440 | tf_op jit(solution)/shard_map/while/body/eval_jaxpr/ppermute | solution.py:21
  489.5 427.0 %while.37 = (s32[]{:T(128)}, bf16[16,8192]{1,0:T(8,128)(2,1)S(1)}, f32[1,147456]{1,0:T(1,128)S(1)}, s32[11]{0:T(128)S(1)}, s32[]{:T(128)}, /*index=5*/pred[]{:T(...) while((s32[]{:T(128)}, bf16[16,8192]{1,0:T(8,128)(2,1)S(1)}, ...), condition=%wide.region_11.12_spmd.clone, body=%wide.region_6.11_spmd.clone.sunk | while | flops 549044800 | bytes 42802872 | solution.py:280
  506.0 19.6 %collective-permute-done.1 = bf16[16,8192]{1,0:T(8,128)(2,1)S(1)} collective-permute-done((bf16[16,8192]{1,0:T(8,128)(2,1)S(1)}, bf16[16,8192]{1,0:T(8,128)(2,1)S(1)}, u32[]{:S(2)}, u32[]{:S(2)}) %collective-permute-start.1) | collective-permute-done | bytes 262176 | tf_op jit(solution)/shard_map/while/body/eval_jaxpr/ppermute | solution.py:21
  532.4 87.0 %collective-permute-done.1 = bf16[16,8192]{1,0:T(8,128)(2,1)S(1)} collective-permute-done((bf16[16,8192]{1,0:T(8,128)(2,1)S(1)}, bf16[16,8192]{1,0:T(8,128)(2,1)S(1)}, u32[]{:S(2)}, u32[]{:S(2)}) %collective-permute-start.1) | collective-permute-done | bytes 262176 | tf_op jit(solution)/shard_map/while/body/eval_jaxpr/ppermute | solution.py:21
  620.7 28.8 %conditional.6 = (bf16[16,8192]{1,0:T(8,128)(2,1)S(1)}, f32[1,131072]{1,0:T(1,128)S(1)}, f32[1,16384]{1,0:T(1,128)S(1)}) conditional(s32[]{:T(128)} %convert_element_type.135, () %tuple.120, (pred[]{:T(512)}, bf16[8,16,8192]{2,1,0:T(8,128)(2,1)}, s32[]{:T(128)}, bf16[16,8192]{1,0:T(8,128)(2,1)S(1)}, f32[8,16,1]{1,2,0:T(1,128)S(1)}, ...), branch_computations={%region_7.7_spmd, %region_8.9_spmd} | conditional | flops 548307520 | bytes 39984272 | solution.py:268
  657.8 28.8 %conditional.6 = (bf16[16,8192]{1,0:T(8,128)(2,1)S(1)}, f32[1,131072]{1,0:T(1,128)S(1)}, f32[1,16384]{1,0:T(1,128)S(1)}) conditional(s32[]{:T(128)} %convert_element_type.135, () %tuple.120, (pred[]{:T(512)}, bf16[8,16,8192]{2,1,0:T(8,128)(2,1)}, s32[]{:T(128)}, bf16[16,8192]{1,0:T(8,128)(2,1)S(1)}, f32[8,16,1]{1,2,0:T(1,128)S(1)}, ...), branch_computations={%region_7.7_spmd, %region_8.9_spmd} | conditional | flops 548307520 | bytes 39984272 | solution.py:268
  694.9 28.8 %conditional.6 = (bf16[16,8192]{1,0:T(8,128)(2,1)S(1)}, f32[1,131072]{1,0:T(1,128)S(1)}, f32[1,16384]{1,0:T(1,128)S(1)}) conditional(s32[]{:T(128)} %convert_element_type.135, () %tuple.120, (pred[]{:T(512)}, bf16[8,16,8192]{2,1,0:T(8,128)(2,1)}, s32[]{:T(128)}, bf16[16,8192]{1,0:T(8,128)(2,1)S(1)}, f32[8,16,1]{1,2,0:T(1,128)S(1)}, ...), branch_computations={%region_7.7_spmd, %region_8.9_spmd} | conditional | flops 548307520 | bytes 39984272 | solution.py:268
  732.1 28.8 %conditional.6 = (bf16[16,8192]{1,0:T(8,128)(2,1)S(1)}, f32[1,131072]{1,0:T(1,128)S(1)}, f32[1,16384]{1,0:T(1,128)S(1)}) conditional(s32[]{:T(128)} %convert_element_type.135, () %tuple.120, (pred[]{:T(512)}, bf16[8,16,8192]{2,1,0:T(8,128)(2,1)}, s32[]{:T(128)}, bf16[16,8192]{1,0:T(8,128)(2,1)S(1)}, f32[8,16,1]{1,2,0:T(1,128)S(1)}, ...), branch_computations={%region_7.7_spmd, %region_8.9_spmd} | conditional | flops 548307520 | bytes 39984272 | solution.py:268
  769.2 28.8 %conditional.6 = (bf16[16,8192]{1,0:T(8,128)(2,1)S(1)}, f32[1,131072]{1,0:T(1,128)S(1)}, f32[1,16384]{1,0:T(1,128)S(1)}) conditional(s32[]{:T(128)} %convert_element_type.135, () %tuple.120, (pred[]{:T(512)}, bf16[8,16,8192]{2,1,0:T(8,128)(2,1)}, s32[]{:T(128)}, bf16[16,8192]{1,0:T(8,128)(2,1)S(1)}, f32[8,16,1]{1,2,0:T(1,128)S(1)}, ...), branch_computations={%region_7.7_spmd, %region_8.9_spmd} | conditional | flops 548307520 | bytes 39984272 | solution.py:268
  806.4 28.8 %conditional.6 = (bf16[16,8192]{1,0:T(8,128)(2,1)S(1)}, f32[1,131072]{1,0:T(1,128)S(1)}, f32[1,16384]{1,0:T(1,128)S(1)}) conditional(s32[]{:T(128)} %convert_element_type.135, () %tuple.120, (pred[]{:T(512)}, bf16[8,16,8192]{2,1,0:T(8,128)(2,1)}, s32[]{:T(128)}, bf16[16,8192]{1,0:T(8,128)(2,1)S(1)}, f32[8,16,1]{1,2,0:T(1,128)S(1)}, ...), branch_computations={%region_7.7_spmd, %region_8.9_spmd} | conditional | flops 548307520 | bytes 39984272 | solution.py:268
  843.5 28.8 %conditional.6 = (bf16[16,8192]{1,0:T(8,128)(2,1)S(1)}, f32[1,131072]{1,0:T(1,128)S(1)}, f32[1,16384]{1,0:T(1,128)S(1)}) conditional(s32[]{:T(128)} %convert_element_type.135, () %tuple.120, (pred[]{:T(512)}, bf16[8,16,8192]{2,1,0:T(8,128)(2,1)}, s32[]{:T(128)}, bf16[16,8192]{1,0:T(8,128)(2,1)S(1)}, f32[8,16,1]{1,2,0:T(1,128)S(1)}, ...), branch_computations={%region_7.7_spmd, %region_8.9_spmd} | conditional | flops 548307520 | bytes 39984272 | solution.py:268
  880.6 28.8 %conditional.6 = (bf16[16,8192]{1,0:T(8,128)(2,1)S(1)}, f32[1,131072]{1,0:T(1,128)S(1)}, f32[1,16384]{1,0:T(1,128)S(1)}) conditional(s32[]{:T(128)} %convert_element_type.135, () %tuple.120, (pred[]{:T(512)}, bf16[8,16,8192]{2,1,0:T(8,128)(2,1)}, s32[]{:T(128)}, bf16[16,8192]{1,0:T(8,128)(2,1)S(1)}, f32[8,16,1]{1,2,0:T(1,128)S(1)}, ...), branch_computations={%region_7.7_spmd, %region_8.9_spmd} | conditional | flops 548307520 | bytes 39984272 | solution.py:268
  926.7 28.0 %all-to-all-start.1 = ((bf16[32,2,4608]{2,1,0:T(2,128)(2,1)}), bf16[32,2,4608]{2,1,0:T(2,128)(2,1)S(1)}, u32[]{:S(2)}, u32[]{:S(2)}) async-start(bf16[32,2,4608]{2,1,0:T(2,128)(2,1)} %reshape.278), calls=%async_computation.1 | async-start | bytes 1179648 | tf_op jit(solution)/shard_map/all_to_all | solution.py:289
  954.9 12.0 %all-to-all-done.1 = bf16[32,2,4608]{2,1,0:T(2,128)(2,1)S(1)} async-done(((bf16[32,2,4608]{2,1,0:T(2,128)(2,1)}), bf16[32,2,4608]{2,1,0:T(2,128)(2,1)S(1)}, u32[]{:S(2)}, u32[]{:S(2)}) %all-to-all-start.1) | async-done | bytes 589856 | tf_op jit(solution)/shard_map/all_to_all | solution.py:289
  (440 shorter events, 601.7 us)
Async XLA Ops:
  7.2 84.4 %all-gather.3.cloned.1.call-start = ((), (), s32[]{:S(2)}) async-start(), calls=%async_computation.3 | async-start | bytes 17301504 | tf_op jit(solution)/shard_map/all_gather | solution.py:146
  7.9 158.0 %all-gather.5.cloned.1.call-start = ((), (), s32[]{:S(2)}) async-start(), calls=%async_computation.4 | async-start | bytes 17301504 | tf_op jit(solution)/shard_map/all_gather | solution.py:147
  15.3 27.1 %all-to-all-start = ((bf16[32,2,4608]{2,1,0:T(2,128)(2,1)}), bf16[32,2,4608]{2,1,0:T(2,128)(2,1)S(1)}, u32[]{:S(2)}, u32[]{:S(2)}) async-start(bf16[32,2,4608]{2,1,0:T(2,128)(2,1)} %reshape.276), calls=%async_computation | async-start | bytes 1179648 | tf_op jit(solution)/shard_map/all_to_all | solution.py:174
  48.6 120.4 %copy-start.2 = (f32[1,8192]{1,0:T(1,128)S(1)}, f32[1,8192]{1,0:T(1,128)}, u32[]{:S(2)}) copy-start(f32[1,8192]{1,0:T(1,128)} %param.24) | copy-start | bytes 98308
  192.6 7.0 collective-permute-start
  223.1 8.9 collective-permute-start
  255.6 8.1 collective-permute-start
  287.2 7.4 collective-permute-start
  318.2 7.1 collective-permute-start
  348.9 7.1 collective-permute-start
  379.5 7.1 collective-permute-start
  410.2 7.1 collective-permute-start
  422.0 26.0 %collective-permute-start = (bf16[16,8192]{1,0:T(8,128)(2,1)S(1)}, bf16[16,8192]{1,0:T(8,128)(2,1)S(1)}, u32[]{:S(2)}, u32[]{:S(2)}) collective-permute-start(bf16[16,8192]{1,0:T(8,128)(2,1)S(1)} %get-tuple-element.992), channel_id=1, source_target_pairs={{0,32},{32,64},{64,96},{1,33},{33,65},{65,97},{2,34},{34,66},{66,9... | collective-permute-start | bytes 786440 | tf_op jit(solution)/shard_map/while/body/eval_jaxpr/ppermute | solution.py:21
  452.7 7.1 collective-permute-start
  464.4 25.1 %collective-permute-start = (bf16[16,8192]{1,0:T(8,128)(2,1)S(1)}, bf16[16,8192]{1,0:T(8,128)(2,1)S(1)}, u32[]{:S(2)}, u32[]{:S(2)}) collective-permute-start(bf16[16,8192]{1,0:T(8,128)(2,1)S(1)} %get-tuple-element.992), channel_id=1, source_target_pairs={{0,32},{32,64},{64,96},{1,33},{33,65},{65,97},{2,34},{34,66},{66,9... | collective-permute-start | bytes 786440 | tf_op jit(solution)/shard_map/while/body/eval_jaxpr/ppermute | solution.py:21
  491.3 8.0 collective-permute-start.1
  500.9 24.8 %collective-permute-start.1 = (bf16[16,8192]{1,0:T(8,128)(2,1)S(1)}, bf16[16,8192]{1,0:T(8,128)(2,1)S(1)}, u32[]{:S(2)}, u32[]{:S(2)}) collective-permute-start(bf16[16,8192]{1,0:T(8,128)(2,1)S(1)} %get-tuple-element.1013), channel_id=1, source_target_pairs={{32,0},{64,32},{96,64},{33,1},{65,33},{97,65},{34,2},{66,34},{98,6... | collective-permute-start | bytes 786440 | tf_op jit(solution)/shard_map/while/body/eval_jaxpr/ppermute | solution.py:21
  527.3 92.2 %collective-permute-start.1 = (bf16[16,8192]{1,0:T(8,128)(2,1)S(1)}, bf16[16,8192]{1,0:T(8,128)(2,1)S(1)}, u32[]{:S(2)}, u32[]{:S(2)}) collective-permute-start(bf16[16,8192]{1,0:T(8,128)(2,1)S(1)} %get-tuple-element.1013), channel_id=1, source_target_pairs={{32,0},{64,32},{96,64},{33,1},{65,33},{97,65},{34,2},{66,34},{98,6... | collective-permute-start | bytes 786440 | tf_op jit(solution)/shard_map/while/body/eval_jaxpr/ppermute | solution.py:21
  649.4 7.1 collective-permute-start.1
  686.6 7.1 collective-permute-start.1
  723.7 7.1 collective-permute-start.1
  760.9 7.1 collective-permute-start.1
  798.0 7.1 collective-permute-start.1
  835.1 7.1 collective-permute-start.1
  872.3 7.1 collective-permute-start.1
  909.4 7.1 collective-permute-start.1
  925.4 43.3 %copy-start.12 = (s32[32]{0:T(128)S(1)}, s32[32]{0:T(128)}, u32[]{:S(2)}) copy-start(s32[32]{0:T(128)} %param.27) | copy-start | bytes 388
  925.4 43.3 %copy-start.14 = (pred[64]{0:T(512)(128)(4,1)S(1)}, pred[64]{0:T(512)(128)(4,1)}, u32[]{:S(2)}) copy-start(pred[64]{0:T(512)(128)(4,1)} %copy-done.13) | copy-start | bytes 196
  925.4 43.3 %copy-start.15 = (pred[64]{0:T(512)(128)(4,1)S(1)}, pred[64]{0:T(512)(128)(4,1)}, u32[]{:S(2)}) copy-start(pred[64]{0:T(512)(128)(4,1)} %get-tuple-element.797) | copy-start | bytes 196
  926.7 42.0 %copy-start.3 = (f32[1,64,9216]{2,1,0:T(8,128)S(1)}, f32[1,64,9216]{2,1,0:T(8,128)}, u32[]{:S(2)}) copy-start(f32[1,64,9216]{2,1,0:T(8,128)} %param.33) | copy-start | bytes 7077892
  926.7 40.3 %all-to-all-start.1 = ((bf16[32,2,4608]{2,1,0:T(2,128)(2,1)}), bf16[32,2,4608]{2,1,0:T(2,128)(2,1)S(1)}, u32[]{:S(2)}, u32[]{:S(2)}) async-start(bf16[32,2,4608]{2,1,0:T(2,128)(2,1)} %reshape.278), calls=%async_computation.1 | async-start | bytes 1179648 | tf_op jit(solution)/shard_map/all_to_all | solution.py:289
  978.7 15.9 %all-to-all-start.2 = ((bf16[32,2,4608]{2,1,0:T(2,128)(2,1)}), bf16[32,2,4608]{2,1,0:T(2,128)(2,1)S(1)}, u32[]{:S(2)}, u32[]{:S(2)}) async-start(bf16[32,2,4608]{2,1,0:T(2,128)(2,1)} %reshape.280), calls=%async_computation.2 | async-start | bytes 1179648 | tf_op jit(solution)/shard_map/all_to_all | solution.py:309
  (26 other events, 295.1 us)
Sparse Core Ops, SparseCore 0:
  10.2 81.2 all-gather.2
  93.8 72.0 all-gather.4
where the time goes:
time: 1020 us; the launch traced here: 1010 us
  matrix products  352 us (35%)
  waiting for transfers between devices  293 us (29%)
  starting transfers between devices  133 us (13%)
  other arithmetic  107 us (10%)
  local copies, waits for them, and re-layouts  89.5 us (9%)
  loops' own time  16.4 us (2%)
  between operations  14.8 us (1%)
    dot_general x32, matrix products, contract_trailing(): lax.dot_general(left, right, (((1,), (1,)), ((), ())), preferred_element_...  176 us
    ppermute x22, waiting for transfers between devices, from_behind(): return lax.ppermute(shard, axis, pairs)  141 us
    ppermute x22, starting transfers between devices, from_behind(): return lax.ppermute(shard, axis, pairs)  91.5 us
    all_gather x1, waiting for transfers between devices, on_device(): lax.all_gather(output_projection_weight, 'dp', axis=1, tiled=True)  74.4 us
    dot_general x8, matrix products, layer_reverse_pass(): jnp.dot(output_gradient, output_complete, preferred_element_type=jnp.floa...  65.1 us
    dot_general x8, matrix products, layer_ahead_pass(): jnp.dot(normalized_rows, value_complete, preferred_element_type=jnp.float32)  64.4 us
    all_gather x1, waiting for transfers between devices, on_device(): lax.all_gather(value_projection_weight, 'dp', axis=1, tiled=True)  42.8 us
    scatter-add x11, other arithmetic, backward_step(): block_grads.at[block_slot_index].add(jnp.where(is_valid, grad_term, 0.0))  33.9 us
  transfers between devices with their start and end apart: 27, of which 27 were waited for; matrix products, arithmetic and copies ran while one was open for 9% of the time, Pallas kernels for 0%

commit v1 on v0

--- a/solution.py
+++ b/solution.py
@@ -144,7 +144,10 @@
     divide_position = hidden_width * ADAPTER_RANK
     value_complete, output_complete = (
         lax.all_gather(value_projection_weight, "dp", axis=1, tiled=True),
-        lax.all_gather(output_projection_weight, "dp", axis=1, tiled=True),
+        jnp.concatenate(
+            lax.all_to_all(jnp.stack([output_projection_weight] * lax.axis_size("dp")), "dp", 0, 0),
+            axis=1,
+        ),
     )
     value_complete = value_complete[0]
     output_complete = output_complete[0]

time: 1020 us -> 1170 us (1.15); the launches traced: 1010 us -> 1170 us
  waiting for transfers between devices: 293 us -> 376 us
  starting transfers between devices: 133 us -> 180 us
  blocking collectives: 0 us -> 26.5 us
    all_to_all x1, waiting for transfers between devices: 15.2 us -> 222 us  [on_device(): lax.all_to_all(jnp.stack([output_projection_weight] * lax.axis_size('dp')...]
    all_gather x1 -> x0, waiting for transfers between devices: 74.4 us -> none  [on_device(): lax.all_gather(output_projection_weight, 'dp', axis=1, tiled=True)]
    all_to_all x1, starting transfers between devices: 28 us -> 81.4 us  [on_device(): lax.all_to_all(outgoing.astype(jnp.bfloat16), 'dp', split_axis=0, concat_...]
    all_gather x1, waiting for transfers between devices: 42.8 us -> 0.01 us  [on_device(): lax.all_gather(value_projection_weight, 'dp', axis=1, tiled=True)]
    all_to_all x0 -> x1, blocking collectives: none -> 26.5 us  [on_device(): lax.all_to_all(hand_out(slot_adapter_params[0]), 'dp', split_axis=0, conc...]
  transfers between devices with their start and end apart: 27 -> 26, of which waited for: 27 -> 25; matrix products, arithmetic and copies ran while one was open for 9% -> 8% of each run, Pallas kernels for 0% -> 0%
where the time goes in v1:
time: 1170 us
  waiting for transfers between devices  376 us (32%)
  matrix products  352 us (30%)
  starting transfers between devices  180 us (15%)
  other arithmetic  106 us (9%)
  local copies, waits for them, and re-layouts  94.6 us (8%)
  blocking collectives  26.5 us (2%)
  loops' own time  16.4 us (1%)
  between operations  14.6 us (1%)
    all_to_all x1, waiting for transfers between devices, on_device(): lax.all_to_all(jnp.stack([output_projection_weight] * lax.axis_size('dp')...  222 us
    dot_general x32, matrix products, contract_trailing(): lax.dot_general(left, right, (((1,), (1,)), ((), ())), preferred_element_...  176 us
    ppermute x22, waiting for transfers between devices, from_behind(): return lax.ppermute(shard, axis, pairs)  136 us
    ppermute x22, starting transfers between devices, from_behind(): return lax.ppermute(shard, axis, pairs)  89.7 us
    all_to_all x1, starting transfers between devices, on_device(): lax.all_to_all(outgoing.astype(jnp.bfloat16), 'dp', split_axis=0, concat_...  81.4 us
    dot_general x8, matrix products, layer_reverse_pass(): jnp.dot(output_gradient, output_complete, preferred_element_type=jnp.floa...  65.1 us
    dot_general x8, matrix products, layer_ahead_pass(): jnp.dot(normalized_rows, value_complete, preferred_element_type=jnp.float32)  64.4 us
    scatter-add x11, other arithmetic, backward_step(): block_grads.at[block_slot_index].add(jnp.where(is_valid, grad_term, 0.0))  33.9 us
  transfers between devices with their start and end apart: 26, of which 25 were waited for; matrix products, arithmetic and copies ran while one was open for 8% of the time, Pallas kernels for 0%

profile of v1, /device:TPU:1, one launch (start us, length us, event | category | flops | bytes accessed | tf_op | source)
XLA Modules:
  0.0 1167.1 jit_solution(436314627104125852)
XLA Ops:
  13.4 26.5 %all_to_all.20 = bf16[32,2,4608]{2,1,0:T(2,128)(2,1)S(1)} all-to-all(bf16[32,2,4608]{2,1,0:T(2,128)(2,1)S(1)} %reshape.279), channel_id=1, replica_groups=mesh['section'=4,'dp'=32] {'dp'}, dimensions={0} | all-to-all | bytes 1179648 | tf_op jit(solution)/shard_map/all_to_all | solution.py:177
  60.2 221.7 %all-to-all-done.1 = bf16[32,1,256,1024]{3,2,1,0:T(8,128)(2,1)} async-done(((bf16[32,1,256,1024]{3,2,1,0:T(8,128)(2,1)}), bf16[32,1,256,1024]{3,2,1,0:T(8,128)(2,1)}, u32[]{:S(2)}, u32[]{:S(2)}) %all-to-all-start.1) | async-done | bytes 16777248 | tf_op jit(solution)/shard_map/all_to_all | solution.py:148
  284.9 314.1 %while.36 = (s32[]{:T(128)}, bf16[16,8192]{1,0:T(8,128)(2,1)S(1)}, bf16[8,16,8192]{2,1,0:T(8,128)(2,1)}, f32[8,16,1]{1,2,0:T(1,128)S(1)}, bf16[8,16,8192]{2,1,0:...) while((s32[]{:T(128)}, bf16[16,8192]{1,0:T(8,128)(2,1)S(1)}, ...), condition=%wide.region_5.6_spmd, body=%wide.region_1.5_spmd.sunk | while | flops 543343104 | bytes 42153352 | solution.py:237
  288.9 19.6 %conditional.5 = (bf16[16,8192]{1,0:T(8,128)(2,1)S(1)}, f32[16,1]{0,1:T(1,128)S(1)}, bf16[16,8192]{1,0:T(8,128)(2,1)S(1)}, bf16[16,16]{1,0:T(8,128)(2,1)}) conditional(s32[]{:T(128)} %convert_element_type.134, () %tuple.117, (bf16[16,8192]{1,0:T(8,128)(2,1)S(1)}, f32[1,8192]{1,0:T(1,128)S(1)}, bf16[8192,1024]{1,0:T(8,128)(2,1)}, ...), branch_computations={%region_2.2_spmd, %region_3.4_spmd} | conditional | flops 542949632 | bytes 37946776 | solution.py:220
  298.2 10.3 fusion
  317.1 19.6 %conditional.5 = (bf16[16,8192]{1,0:T(8,128)(2,1)S(1)}, f32[16,1]{0,1:T(1,128)S(1)}, bf16[16,8192]{1,0:T(8,128)(2,1)S(1)}, bf16[16,16]{1,0:T(8,128)(2,1)}) conditional(s32[]{:T(128)} %convert_element_type.134, () %tuple.117, (bf16[16,8192]{1,0:T(8,128)(2,1)S(1)}, f32[1,8192]{1,0:T(1,128)S(1)}, bf16[8192,1024]{1,0:T(8,128)(2,1)}, ...), branch_computations={%region_2.2_spmd, %region_3.4_spmd} | conditional | flops 542949632 | bytes 37946776 | solution.py:220
  326.3 10.3 fusion
  347.8 19.6 %conditional.5 = (bf16[16,8192]{1,0:T(8,128)(2,1)S(1)}, f32[16,1]{0,1:T(1,128)S(1)}, bf16[16,8192]{1,0:T(8,128)(2,1)S(1)}, bf16[16,16]{1,0:T(8,128)(2,1)}) conditional(s32[]{:T(128)} %convert_element_type.134, () %tuple.117, (bf16[16,8192]{1,0:T(8,128)(2,1)S(1)}, f32[1,8192]{1,0:T(1,128)S(1)}, bf16[8192,1024]{1,0:T(8,128)(2,1)}, ...), branch_computations={%region_2.2_spmd, %region_3.4_spmd} | conditional | flops 542949632 | bytes 37946776 | solution.py:220
  357.0 10.3 fusion
  378.4 19.6 %conditional.5 = (bf16[16,8192]{1,0:T(8,128)(2,1)S(1)}, f32[16,1]{0,1:T(1,128)S(1)}, bf16[16,8192]{1,0:T(8,128)(2,1)S(1)}, bf16[16,16]{1,0:T(8,128)(2,1)}) conditional(s32[]{:T(128)} %convert_element_type.134, () %tuple.117, (bf16[16,8192]{1,0:T(8,128)(2,1)S(1)}, f32[1,8192]{1,0:T(1,128)S(1)}, bf16[8192,1024]{1,0:T(8,128)(2,1)}, ...), branch_computations={%region_2.2_spmd, %region_3.4_spmd} | conditional | flops 542949632 | bytes 37946776 | solution.py:220
  387.7 10.3 fusion
  409.1 19.6 %conditional.5 = (bf16[16,8192]{1,0:T(8,128)(2,1)S(1)}, f32[16,1]{0,1:T(1,128)S(1)}, bf16[16,8192]{1,0:T(8,128)(2,1)S(1)}, bf16[16,16]{1,0:T(8,128)(2,1)}) conditional(s32[]{:T(128)} %convert_element_type.134, () %tuple.117, (bf16[16,8192]{1,0:T(8,128)(2,1)S(1)}, f32[1,8192]{1,0:T(1,128)S(1)}, bf16[8192,1024]{1,0:T(8,128)(2,1)}, ...), branch_computations={%region_2.2_spmd, %region_3.4_spmd} | conditional | flops 542949632 | bytes 37946776 | solution.py:220
  418.3 10.3 fusion
  439.8 19.6 %conditional.5 = (bf16[16,8192]{1,0:T(8,128)(2,1)S(1)}, f32[16,1]{0,1:T(1,128)S(1)}, bf16[16,8192]{1,0:T(8,128)(2,1)S(1)}, bf16[16,16]{1,0:T(8,128)(2,1)}) conditional(s32[]{:T(128)} %convert_element_type.134, () %tuple.117, (bf16[16,8192]{1,0:T(8,128)(2,1)S(1)}, f32[1,8192]{1,0:T(1,128)S(1)}, bf16[8192,1024]{1,0:T(8,128)(2,1)}, ...), branch_computations={%region_2.2_spmd, %region_3.4_spmd} | conditional | flops 542949632 | bytes 37946776 | solution.py:220
  449.0 10.3 fusion
  470.5 19.6 %conditional.5 = (bf16[16,8192]{1,0:T(8,128)(2,1)S(1)}, f32[16,1]{0,1:T(1,128)S(1)}, bf16[16,8192]{1,0:T(8,128)(2,1)S(1)}, bf16[16,16]{1,0:T(8,128)(2,1)}) conditional(s32[]{:T(128)} %convert_element_type.134, () %tuple.117, (bf16[16,8192]{1,0:T(8,128)(2,1)S(1)}, f32[1,8192]{1,0:T(1,128)S(1)}, bf16[8192,1024]{1,0:T(8,128)(2,1)}, ...), branch_computations={%region_2.2_spmd, %region_3.4_spmd} | conditional | flops 542949632 | bytes 37946776 | solution.py:220
  501.1 19.6 %conditional.5 = (bf16[16,8192]{1,0:T(8,128)(2,1)S(1)}, f32[16,1]{0,1:T(1,128)S(1)}, bf16[16,8192]{1,0:T(8,128)(2,1)S(1)}, bf16[16,16]{1,0:T(8,128)(2,1)}) conditional(s32[]{:T(128)} %convert_element_type.134, () %tuple.117, (bf16[16,8192]{1,0:T(8,128)(2,1)S(1)}, f32[1,8192]{1,0:T(1,128)S(1)}, bf16[8192,1024]{1,0:T(8,128)(2,1)}, ...), branch_computations={%region_2.2_spmd, %region_3.4_spmd} | conditional | flops 542949632 | bytes 37946776 | solution.py:220
  532.5 22.8 %collective-permute-start = (bf16[16,8192]{1,0:T(8,128)(2,1)S(1)}, bf16[16,8192]{1,0:T(8,128)(2,1)S(1)}, u32[]{:S(2)}, u32[]{:S(2)}) collective-permute-start(bf16[16,8192]{1,0:T(8,128)(2,1)S(1)} %get-tuple-element.992), channel_id=1, source_target_pairs={{0,32},{32,64},{64,96},{1,33},{33,65},{65,97},{2,34},{34,66},{66,9... | collective-permute-start | bytes 786440 | tf_op jit(solution)/shard_map/while/body/eval_jaxpr/ppermute | solution.py:21
  574.9 20.9 %collective-permute-start = (bf16[16,8192]{1,0:T(8,128)(2,1)S(1)}, bf16[16,8192]{1,0:T(8,128)(2,1)S(1)}, u32[]{:S(2)}, u32[]{:S(2)}) collective-permute-start(bf16[16,8192]{1,0:T(8,128)(2,1)S(1)} %get-tuple-element.992), channel_id=1, source_target_pairs={{0,32},{32,64},{64,96},{1,33},{33,65},{65,97},{2,34},{34,66},{66,9... | collective-permute-start | bytes 786440 | tf_op jit(solution)/shard_map/while/body/eval_jaxpr/ppermute | solution.py:21
  599.1 426.6 %while.37 = (s32[]{:T(128)}, bf16[16,8192]{1,0:T(8,128)(2,1)S(1)}, f32[1,147456]{1,0:T(1,128)S(1)}, s32[11]{0:T(128)S(1)}, s32[]{:T(128)}, /*index=5*/pred[]{:T(...) while((s32[]{:T(128)}, bf16[16,8192]{1,0:T(8,128)(2,1)S(1)}, ...), condition=%wide.region_11.12_spmd.clone, body=%wide.region_6.11_spmd.clone.sunk | while | flops 549044800 | bytes 42802872 | solution.py:283
  615.2 19.7 %collective-permute-done.1 = bf16[16,8192]{1,0:T(8,128)(2,1)S(1)} collective-permute-done((bf16[16,8192]{1,0:T(8,128)(2,1)S(1)}, bf16[16,8192]{1,0:T(8,128)(2,1)S(1)}, u32[]{:S(2)}, u32[]{:S(2)}) %collective-permute-start.1) | collective-permute-done | bytes 262176 | tf_op jit(solution)/shard_map/while/body/eval_jaxpr/ppermute | solution.py:21
  641.6 86.8 %collective-permute-done.1 = bf16[16,8192]{1,0:T(8,128)(2,1)S(1)} collective-permute-done((bf16[16,8192]{1,0:T(8,128)(2,1)S(1)}, bf16[16,8192]{1,0:T(8,128)(2,1)S(1)}, u32[]{:S(2)}, u32[]{:S(2)}) %collective-permute-start.1) | collective-permute-done | bytes 262176 | tf_op jit(solution)/shard_map/while/body/eval_jaxpr/ppermute | solution.py:21
  729.7 28.8 %conditional.6 = (bf16[16,8192]{1,0:T(8,128)(2,1)S(1)}, f32[1,131072]{1,0:T(1,128)S(1)}, f32[1,16384]{1,0:T(1,128)S(1)}) conditional(s32[]{:T(128)} %convert_element_type.135, () %tuple.120, (pred[]{:T(512)}, bf16[8,16,8192]{2,1,0:T(8,128)(2,1)}, s32[]{:T(128)}, bf16[16,8192]{1,0:T(8,128)(2,1)S(1)}, f32[8,16,1]{1,2,0:T(1,128)S(1)}, ...), branch_computations={%region_7.7_spmd, %region_8.9_spmd} | conditional | flops 548307520 | bytes 39984272 | solution.py:271
  766.9 28.8 %conditional.6 = (bf16[16,8192]{1,0:T(8,128)(2,1)S(1)}, f32[1,131072]{1,0:T(1,128)S(1)}, f32[1,16384]{1,0:T(1,128)S(1)}) conditional(s32[]{:T(128)} %convert_element_type.135, () %tuple.120, (pred[]{:T(512)}, bf16[8,16,8192]{2,1,0:T(8,128)(2,1)}, s32[]{:T(128)}, bf16[16,8192]{1,0:T(8,128)(2,1)S(1)}, f32[8,16,1]{1,2,0:T(1,128)S(1)}, ...), branch_computations={%region_7.7_spmd, %region_8.9_spmd} | conditional | flops 548307520 | bytes 39984272 | solution.py:271
  804.0 28.8 %conditional.6 = (bf16[16,8192]{1,0:T(8,128)(2,1)S(1)}, f32[1,131072]{1,0:T(1,128)S(1)}, f32[1,16384]{1,0:T(1,128)S(1)}) conditional(s32[]{:T(128)} %convert_element_type.135, () %tuple.120, (pred[]{:T(512)}, bf16[8,16,8192]{2,1,0:T(8,128)(2,1)}, s32[]{:T(128)}, bf16[16,8192]{1,0:T(8,128)(2,1)S(1)}, f32[8,16,1]{1,2,0:T(1,128)S(1)}, ...), branch_computations={%region_7.7_spmd, %region_8.9_spmd} | conditional | flops 548307520 | bytes 39984272 | solution.py:271
  841.1 28.8 %conditional.6 = (bf16[16,8192]{1,0:T(8,128)(2,1)S(1)}, f32[1,131072]{1,0:T(1,128)S(1)}, f32[1,16384]{1,0:T(1,128)S(1)}) conditional(s32[]{:T(128)} %convert_element_type.135, () %tuple.120, (pred[]{:T(512)}, bf16[8,16,8192]{2,1,0:T(8,128)(2,1)}, s32[]{:T(128)}, bf16[16,8192]{1,0:T(8,128)(2,1)S(1)}, f32[8,16,1]{1,2,0:T(1,128)S(1)}, ...), branch_computations={%region_7.7_spmd, %region_8.9_spmd} | conditional | flops 548307520 | bytes 39984272 | solution.py:271
  878.3 28.8 %conditional.6 = (bf16[16,8192]{1,0:T(8,128)(2,1)S(1)}, f32[1,131072]{1,0:T(1,128)S(1)}, f32[1,16384]{1,0:T(1,128)S(1)}) conditional(s32[]{:T(128)} %convert_element_type.135, () %tuple.120, (pred[]{:T(512)}, bf16[8,16,8192]{2,1,0:T(8,128)(2,1)}, s32[]{:T(128)}, bf16[16,8192]{1,0:T(8,128)(2,1)S(1)}, f32[8,16,1]{1,2,0:T(1,128)S(1)}, ...), branch_computations={%region_7.7_spmd, %region_8.9_spmd} | conditional | flops 548307520 | bytes 39984272 | solution.py:271
  915.4 28.8 %conditional.6 = (bf16[16,8192]{1,0:T(8,128)(2,1)S(1)}, f32[1,131072]{1,0:T(1,128)S(1)}, f32[1,16384]{1,0:T(1,128)S(1)}) conditional(s32[]{:T(128)} %convert_element_type.135, () %tuple.120, (pred[]{:T(512)}, bf16[8,16,8192]{2,1,0:T(8,128)(2,1)}, s32[]{:T(128)}, bf16[16,8192]{1,0:T(8,128)(2,1)S(1)}, f32[8,16,1]{1,2,0:T(1,128)S(1)}, ...), branch_computations={%region_7.7_spmd, %region_8.9_spmd} | conditional | flops 548307520 | bytes 39984272 | solution.py:271
  952.6 28.8 %conditional.6 = (bf16[16,8192]{1,0:T(8,128)(2,1)S(1)}, f32[1,131072]{1,0:T(1,128)S(1)}, f32[1,16384]{1,0:T(1,128)S(1)}) conditional(s32[]{:T(128)} %convert_element_type.135, () %tuple.120, (pred[]{:T(512)}, bf16[8,16,8192]{2,1,0:T(8,128)(2,1)}, s32[]{:T(128)}, bf16[16,8192]{1,0:T(8,128)(2,1)S(1)}, f32[8,16,1]{1,2,0:T(1,128)S(1)}, ...), branch_computations={%region_7.7_spmd, %region_8.9_spmd} | conditional | flops 548307520 | bytes 39984272 | solution.py:271
  989.7 28.8 %conditional.6 = (bf16[16,8192]{1,0:T(8,128)(2,1)S(1)}, f32[1,131072]{1,0:T(1,128)S(1)}, f32[1,16384]{1,0:T(1,128)S(1)}) conditional(s32[]{:T(128)} %convert_element_type.135, () %tuple.120, (pred[]{:T(512)}, bf16[8,16,8192]{2,1,0:T(8,128)(2,1)}, s32[]{:T(128)}, bf16[16,8192]{1,0:T(8,128)(2,1)S(1)}, f32[8,16,1]{1,2,0:T(1,128)S(1)}, ...), branch_computations={%region_7.7_spmd, %region_8.9_spmd} | conditional | flops 548307520 | bytes 39984272 | solution.py:271
  1035.7 81.4 %all-to-all-start.2 = ((bf16[32,2,4608]{2,1,0:T(2,128)(2,1)}), bf16[32,2,4608]{2,1,0:T(2,128)(2,1)S(1)}, u32[]{:S(2)}, u32[]{:S(2)}) async-start(bf16[32,2,4608]{2,1,0:T(2,128)(2,1)} %reshape.281), calls=%async_computation.2 | async-start | bytes 1179648 | tf_op jit(solution)/shard_map/all_to_all | solution.py:292
  1117.2 12.0 %all-to-all-done.2 = bf16[32,2,4608]{2,1,0:T(2,128)(2,1)S(1)} async-done(((bf16[32,2,4608]{2,1,0:T(2,128)(2,1)}), bf16[32,2,4608]{2,1,0:T(2,128)(2,1)S(1)}, u32[]{:S(2)}, u32[]{:S(2)}) %all-to-all-start.2) | async-done | bytes 589856 | tf_op jit(solution)/shard_map/all_to_all | solution.py:292
  (441 shorter events, 585.5 us)
Async XLA Ops:
  7.2 274.7 %all-gather.2.cloned.1.call-start = ((), (), s32[]{:S(2)}) async-start(), calls=%async_computation.4 | async-start | bytes 17301504 | tf_op jit(solution)/shard_map/all_gather | solution.py:146
  46.0 235.9 %all-to-all-start.1 = ((bf16[32,1,256,1024]{3,2,1,0:T(8,128)(2,1)}), bf16[32,1,256,1024]{3,2,1,0:T(8,128)(2,1)}, u32[]{:S(2)}, u32[]{:S(2)}) async-start(bf16[32,1,256,1024]{3,2,1,0:T(8,128)(2,1)} %stack.2), calls=%async_computation.1 | async-start | bytes 33554432 | tf_op jit(solution)/shard_map/all_to_all | solution.py:148
  59.9 225.0 %copy-start.2 = (f32[1,8192]{1,0:T(1,128)S(1)}, f32[1,8192]{1,0:T(1,128)}, u32[]{:S(2)}) copy-start(f32[1,8192]{1,0:T(1,128)} %param.24) | copy-start | bytes 98308
  308.5 4.6 collective-permute-start
  336.7 7.1 collective-permute-start
  367.3 7.1 collective-permute-start
  398.0 7.1 collective-permute-start
  428.7 7.1 collective-permute-start
  459.4 7.1 collective-permute-start
  490.0 7.1 collective-permute-start
  520.7 7.1 collective-permute-start
  532.5 26.0 %collective-permute-start = (bf16[16,8192]{1,0:T(8,128)(2,1)S(1)}, bf16[16,8192]{1,0:T(8,128)(2,1)S(1)}, u32[]{:S(2)}, u32[]{:S(2)}) collective-permute-start(bf16[16,8192]{1,0:T(8,128)(2,1)S(1)} %get-tuple-element.992), channel_id=1, source_target_pairs={{0,32},{32,64},{64,96},{1,33},{33,65},{65,97},{2,34},{34,66},{66,9... | collective-permute-start | bytes 786440 | tf_op jit(solution)/shard_map/while/body/eval_jaxpr/ppermute | solution.py:21
  563.1 7.1 collective-permute-start
  574.9 24.1 %collective-permute-start = (bf16[16,8192]{1,0:T(8,128)(2,1)S(1)}, bf16[16,8192]{1,0:T(8,128)(2,1)S(1)}, u32[]{:S(2)}, u32[]{:S(2)}) collective-permute-start(bf16[16,8192]{1,0:T(8,128)(2,1)S(1)} %get-tuple-element.992), channel_id=1, source_target_pairs={{0,32},{32,64},{64,96},{1,33},{33,65},{65,97},{2,34},{34,66},{66,9... | collective-permute-start | bytes 786440 | tf_op jit(solution)/shard_map/while/body/eval_jaxpr/ppermute | solution.py:21
  600.9 7.6 collective-permute-start.1
  610.0 24.8 %collective-permute-start.1 = (bf16[16,8192]{1,0:T(8,128)(2,1)S(1)}, bf16[16,8192]{1,0:T(8,128)(2,1)S(1)}, u32[]{:S(2)}, u32[]{:S(2)}) collective-permute-start(bf16[16,8192]{1,0:T(8,128)(2,1)S(1)} %get-tuple-element.1013), channel_id=1, source_target_pairs={{32,0},{64,32},{96,64},{33,1},{65,33},{97,65},{34,2},{66,34},{98,6... | collective-permute-start | bytes 786440 | tf_op jit(solution)/shard_map/while/body/eval_jaxpr/ppermute | solution.py:21
  636.5 92.0 %collective-permute-start.1 = (bf16[16,8192]{1,0:T(8,128)(2,1)S(1)}, bf16[16,8192]{1,0:T(8,128)(2,1)S(1)}, u32[]{:S(2)}, u32[]{:S(2)}) collective-permute-start(bf16[16,8192]{1,0:T(8,128)(2,1)S(1)} %get-tuple-element.1013), channel_id=1, source_target_pairs={{32,0},{64,32},{96,64},{33,1},{65,33},{97,65},{34,2},{66,34},{98,6... | collective-permute-start | bytes 786440 | tf_op jit(solution)/shard_map/while/body/eval_jaxpr/ppermute | solution.py:21
  758.5 7.1 collective-permute-start.1
  795.6 7.1 collective-permute-start.1
  832.8 7.1 collective-permute-start.1
  869.9 7.1 collective-permute-start.1
  907.1 7.1 collective-permute-start.1
  944.2 7.1 collective-permute-start.1
  981.4 7.1 collective-permute-start.1
  1018.5 7.1 collective-permute-start.1
  1033.3 83.7 %copy-start.11 = (s32[64]{0:T(128)S(1)}, s32[64]{0:T(128)}, u32[]{:S(2)}) copy-start(s32[64]{0:T(128)} %copy-done.10) | copy-start | bytes 772
  1034.4 96.7 %copy-start.13 = (s32[32]{0:T(128)S(1)}, s32[32]{0:T(128)}, u32[]{:S(2)}) copy-start(s32[32]{0:T(128)} %param.27) | copy-start | bytes 388
  1034.4 96.7 %copy-start.15 = (pred[64]{0:T(512)(128)(4,1)S(1)}, pred[64]{0:T(512)(128)(4,1)}, u32[]{:S(2)}) copy-start(pred[64]{0:T(512)(128)(4,1)} %copy-done.14) | copy-start | bytes 196
  1034.4 96.7 %copy-start.16 = (pred[64]{0:T(512)(128)(4,1)S(1)}, pred[64]{0:T(512)(128)(4,1)}, u32[]{:S(2)}) copy-start(pred[64]{0:T(512)(128)(4,1)} %get-tuple-element.797) | copy-start | bytes 196
  1035.7 95.4 %copy-start.3 = (f32[1,64,9216]{2,1,0:T(8,128)S(1)}, f32[1,64,9216]{2,1,0:T(8,128)}, u32[]{:S(2)}) copy-start(f32[1,64,9216]{2,1,0:T(8,128)} %param.33) | copy-start | bytes 7077892
  1035.7 93.6 %all-to-all-start.2 = ((bf16[32,2,4608]{2,1,0:T(2,128)(2,1)}), bf16[32,2,4608]{2,1,0:T(2,128)(2,1)S(1)}, u32[]{:S(2)}, u32[]{:S(2)}) async-start(bf16[32,2,4608]{2,1,0:T(2,128)(2,1)} %reshape.281), calls=%async_computation.2 | async-start | bytes 1179648 | tf_op jit(solution)/shard_map/all_to_all | solution.py:292
  1141.0 15.9 %all-to-all-start.3 = ((bf16[32,2,4608]{2,1,0:T(2,128)(2,1)}), bf16[32,2,4608]{2,1,0:T(2,128)(2,1)S(1)}, u32[]{:S(2)}, u32[]{:S(2)}) async-start(bf16[32,2,4608]{2,1,0:T(2,128)(2,1)} %reshape.283), calls=%async_computation.3 | async-start | bytes 1179648 | tf_op jit(solution)/shard_map/all_to_all | solution.py:312
  (26 other events, 357.7 us)
Sparse Core Ops, SparseCore 0:
  10.2 242.9 all-gather.1
